TPU v7x, 128 devices: a whole 4x4x4 slice. The times are simulated.
128 devices in a mesh: ctx: 16 (over z, x_lo, core), tp: 8 (over x_hi, y).
Axes of the slice: x: 4 (x_hi: 2, x_lo: 2; x = x_hi * 2 + x_lo), y: 4, z: 4, core: 2. Of those that a mesh axis runs over, the one named last changes fastest.
Arguments:
- hidden_in: bfloat16 [16384, 5376], P(('ctx', 'tp')), may hold values from -6 to 6
- in_gain: float32 [5376], replicated, may hold values from 0.1 to 1.9
- query_weight: bfloat16 [5376, 4096], P('ctx', 'tp'), may hold values from -0.078125 to 0.078125
- key_weight: bfloat16 [5376, 2048], P('ctx', 'tp'), may hold values from -0.078125 to 0.078125
- value_weight: bfloat16 [5376, 2048], P('ctx', 'tp'), may hold values from -0.078125 to 0.078125
- out_weight: bfloat16 [4096, 5376], P('tp', 'ctx'), may hold values from -0.09375 to 0.09375
- q_gain: float32 [128], replicated, may hold values from 0.5 to 16
- k_gain: float32 [128], replicated, may hold values from 0.5 to 16
- post_gain: float32 [5376], replicated, may hold values from 0.1 to 1.9
Outputs:
- layer_out: bfloat16 [16384, 5376], P(('ctx', 'tp'))
All inputs are finite; a program needn't handle non-finite values.
Results may differ from a plain program's by a relative error of at most 0.015.
The roundings to bfloat16 on the way count: a program that leaves them out, or rounds other values in their place, can miss the bound.
Values may be sent and summed in bfloat16 or wider, within the bound.
A program may use at most 192 MiB of HBM per device.

v0:
```python
import jax
import jax.numpy as jnp
from jax import lax
from jax.sharding import PartitionSpec as P

WINDOW = 1024
SCALAR = 168


def from_behind(array, axis, by):
    peers = lax.axis_size(axis)
    pairs = [(i, i + by) for i in range(peers) if 0 <= i + by < peers]
    return lax.ppermute(array, axis, pairs)


def rms_scale(values, gain):
    return values * lax.rsqrt(jnp.mean(values * values, axis=-1, keepdims=True) + 1e-06) * gain


def rotate(vectors, positions):
    half_dim = vectors.shape[-1] // 2
    frequency = 10000.0 ** (-(jnp.arange(half_dim, dtype=jnp.float32) * 2.0 / vectors.shape[-1]))
    angles = positions.astype(jnp.float32)[:, None] * frequency[None, :]
    cosine = jnp.cos(angles)[:, None, :]
    sine_part = jnp.sin(angles)[:, None, :]
    first_half = vectors[..., :half_dim]
    second_half = vectors[..., half_dim:]
    return jnp.concatenate(
        [
            first_half * cosine - second_half * sine_part,
            second_half * cosine + first_half * sine_part,
        ],
        axis=-1,
    )


def attend(queries, keys, values, query_pos, key_pos):
    row_count, query_heads, head_dim = queries.shape
    key_heads = keys.shape[1]
    group_size = query_heads // key_heads
    grouped = queries.reshape(row_count, key_heads, group_size, head_dim)
    scores = jnp.einsum("rhgd,khd->hgrk", grouped, keys, preferred_element_type=jnp.float32)
    offset = query_pos[:, None] - key_pos[None, :]
    allowed = (offset >= 0) & (offset < WINDOW) & (key_pos[None, :] >= 0)
    scores = jnp.where(allowed, scores * float(SCALAR) ** (-0.5), -1e30)
    row_max = jnp.max(scores, axis=-1, keepdims=True)
    expo = jnp.where(allowed, jnp.exp(scores - row_max), 0.0)
    weights = (expo / jnp.sum(expo, axis=-1, keepdims=True)).astype(jnp.bfloat16)
    mixed = jnp.einsum("hgrk,khd->rhgd", weights, values, preferred_element_type=jnp.float32)
    return mixed.astype(jnp.bfloat16).reshape(row_count, query_heads * head_dim)


def attend_blocks(queries, keys, values, query_pos, key_pos):
    row_count = queries.shape[0]
    piece_rows = min(row_count, 512)
    outputs = []
    for first in range(0, row_count, piece_rows):
        outputs.append(
            attend(
                queries[first : first + piece_rows],
                keys[first : first + piece_rows + WINDOW],
                values[first : first + piece_rows + WINDOW],
                query_pos[first : first + piece_rows],
                key_pos[first : first + piece_rows + WINDOW],
            )
        )
    return jnp.concatenate(outputs, axis=0)


def add_product(left, weight_piece):
    return jnp.dot(left, weight_piece, preferred_element_type=jnp.float32)


def reach_keys(keys, values):
    got_keys, got_values = from_behind((keys, values), "ctx", 1)
    far_keys = [got_keys]
    far_values = [got_values]
    return (
        jnp.concatenate(far_keys + [keys], axis=0),
        jnp.concatenate(far_values + [values], axis=0),
    )


def per_device(
    hidden_in,
    in_gain,
    query_weight,
    key_weight,
    value_weight,
    out_weight,
    q_gain,
    k_gain,
    post_gain,
):
    normed = rms_scale(hidden_in.astype(jnp.float32), in_gain).astype(jnp.bfloat16)
    block = lax.all_gather(normed, "tp", axis=0, tiled=True)
    block_rows = block.shape[0]
    head_dim = q_gain.shape[0]
    block_start = lax.axis_index("ctx") * block_rows
    own_pos = block_start + jnp.arange(block_rows, dtype=jnp.int32)
    wide_pos = block_start - WINDOW + jnp.arange(WINDOW + block_rows, dtype=jnp.int32)
    kv_rows = block.shape[0]
    query_raw = add_product(block, lax.all_gather(query_weight, "ctx", axis=0, tiled=True))
    key_raw = add_product(block, lax.all_gather(key_weight, "ctx", axis=0, tiled=True))
    value_raw = add_product(block, lax.all_gather(value_weight, "ctx", axis=0, tiled=True))
    queries = rotate(
        rms_scale(query_raw.reshape(block_rows, -1, head_dim), q_gain), own_pos
    ).astype(jnp.bfloat16)
    keys = rotate(rms_scale(key_raw.reshape(kv_rows, -1, head_dim), k_gain), own_pos).astype(
        jnp.bfloat16
    )
    values = value_raw.astype(jnp.bfloat16).reshape(kv_rows, -1, head_dim)
    keys, values = reach_keys(keys, values)
    attended = attend_blocks(queries, keys, values, own_pos, wide_pos)
    out_full = lax.all_gather(out_weight, "ctx", axis=1, tiled=True)
    projected = lax.psum_scatter(
        jnp.dot(attended, out_full, preferred_element_type=jnp.float32).astype(jnp.bfloat16),
        "tp",
        scatter_dimension=0,
        tiled=True,
    ).astype(jnp.float32)
    return (hidden_in.astype(jnp.float32) + rms_scale(projected, post_gain)).astype(jnp.bfloat16)


def solution(mesh):
    in_specs = (
        P(("ctx", "tp"), None),
        P(),
        P("ctx", "tp"),
        P("ctx", "tp"),
        P("ctx", "tp"),
        P("tp", "ctx"),
        P(),
        P(),
        P(),
    )
    out_specs = P(("ctx", "tp"), None)
    return jax.shard_map(
        per_device, mesh=mesh, in_specs=in_specs, out_specs=out_specs, check_vma=False
    )
```

profile of v0, /device:TPU:0, one launch (start us, length us, event | category | flops | bytes accessed | tf_op | source)
XLA Modules:
  0.0 467.0 jit_solution(9747930731905477069)
XLA Ops:
  6.5 0.7 all-gather.10.cloned.1.call-update
  7.3 1.7 fusion.18
  9.0 2.8 fusion.20
  11.9 0.7 all-gather.8.cloned.1.call-update
  12.6 0.5 all-gather.12.cloned.1.call-update
  13.2 0.5 all-gather.14.cloned.1.call-update
  13.9 1.0 multiply_cosine_fusion
  15.3 1.2 fusion.13
  16.5 2.0 fusion.15
  18.5 28.1 %all-gather.10.cloned.1.call-done = bf16[5376,256]{1,0:T(8,128)(2,1)} async-done(((bf16[336,256]{1,0:T(8,128)(2,1)}), bf16[5376,256]{1,0:T(8,128)(2,1)}) %all-gather.10.cloned.1.call-update) | async-done | bytes 2752528 | tf_op jit(solution)/shard_map/all_gather | solution.py:104
  46.5 132.4 %all-gather.6.cloned.1.call-done = bf16[1024,5376]{1,0:T(8,128)(2,1)} async-done(((bf16[128,5376]{1,0:T(8,128)(2,1)}), bf16[1024,5376]{1,0:T(8,128)(2,1)}) %all-gather.6.cloned.1.call-update) | async-done | bytes 11010064 | tf_op jit(solution)/shard_map/all_gather | solution.py:96
  178.9 9.0 %multiply_reduce_fusion.1 = (f32[1024,2]{0,1:T(2,128)S(1)}, f32[1024,256]{0,1:T(8,128)}) fusion(bf16[1024,5376]{1,0:T(8,128)(2,1)} %all-gather.6.cloned.1.call-done, bf16[5376,256]{1,0:T(8,128)(2,1)} %all-gather.10.cloned.1.call-done), kind=kOutput, calls=%fused_computation.58 | convolution fusion | flops 2819094528 | bytes 14819328 | tf_op jit(solution)/shard_map/dot_general | solution.py:71
  187.9 1.5 copy.17
  189.8 0.5 subtract_convert_fusion.1
  190.3 1.1 pad_maximum_fusion.2
  191.4 1.3 collective-permute-start.1
  192.7 24.8 %all-gather.8.cloned.1.call-done = bf16[5376,256]{1,0:T(8,128)(2,1)} async-done(((bf16[336,256]{1,0:T(8,128)(2,1)}), bf16[5376,256]{1,0:T(8,128)(2,1)}) %all-gather.8.cloned.1.call-update) | async-done | bytes 2752528 | tf_op jit(solution)/shard_map/all_gather | solution.py:105
  217.6 8.8 %convolution_convert_fusion.1 = bf16[1024,256]{0,1:T(8,128)(2,1)} fusion(bf16[1024,5376]{1,0:T(8,128)(2,1)} %all-gather.6.cloned.1.call-done, bf16[5376,256]{1,0:T(8,128)(2,1)} %all-gather.8.cloned.1.call-done), kind=kOutput, calls=%fused_computation.44 | convolution fusion | flops 2818834432 | bytes 14286848 | tf_op jit(solution)/shard_map/dot_general | solution.py:71
  226.3 3.1 collective-permute-start
  229.4 35.3 %all-gather.12.cloned.1.call-done = bf16[5376,512]{1,0:T(8,128)(2,1)} async-done(((bf16[336,512]{1,0:T(8,128)(2,1)}), bf16[5376,512]{1,0:T(8,128)(2,1)}) %all-gather.12.cloned.1.call-update) | async-done | bytes 5505040 | tf_op jit(solution)/shard_map/all_gather | solution.py:103
  264.7 10.3 %multiply_reduce_fusion = (f32[1024,4]{0,1:T(4,128)S(1)}, f32[1024,512]{0,1:T(8,128)S(1)}) fusion(bf16[1024,5376]{1,0:T(8,128)(2,1)} %all-gather.6.cloned.1.call-done, bf16[5376,512]{1,0:T(8,128)(2,1)} %all-gather.12.cloned.1.call-done), kind=kOutput, calls=%fused_computation.39 | convolution fusion | flops 5638189056 | bytes 18628608 | tf_op jit(solution)/shard_map/dot_general | solution.py:71
  275.1 0.5 multiply_multiply_fusion
  275.9 1.1 fusion.39
  277.3 9.5 %fusion.51 = (f32[2,2,512]{2,1,0:T(2,128)S(1)}, f32[2,2,512,1536]{2,3,1,0:T(8,128)}) fusion(pred[512,1536]{0,1:T(8,128)(4,1)S(1)} %fusion.13, bf16[512,2,2,128]{0,3,2,1:T(8,128)(2,1)} %bitcast.89, bf16[2048,2,128]{2,0,1:T(8,128)(2,1)S(1)} %maximum_maximum_fusion), kind=kOutput, calls=%fused_computation.93 | convolution fusion | flops 821036544 | bytes 15474688 | tf_op jit(solution)/shard_map/sub | solution.py:47
  286.8 8.3 %fusion.50 = (f32[2,2,512]{2,1,0:T(2,128)S(1)}, f32[2,2,512,1536]{2,3,1,0:T(8,128)}) fusion(pred[512,1536]{0,1:T(8,128)(4,1)S(1)} %copy-done.1, bf16[512,2,2,128]{0,3,2,1:T(8,128)(2,1)S(1)} %bitcast.88, bf16[2048,2,128]{2,0,1:T(8,128)(2,1)S(1)} %maximum_maximum_fusion), kind=kOutput, calls=%fused_computation.92 | convolution fusion | flops 821036544 | bytes 15474688 | tf_op jit(solution)/shard_map/sub | solution.py:47
  295.1 6.2 %fusion.26 = bf16[2,128,2,512]{3,1,2,0:T(8,128)(2,1)S(1)} fusion(f32[2,2,512,1536]{2,3,1,0:T(8,128)} %get-tuple-element.24, f32[2,2,512]{2,1,0:T(2,128)S(1)} %get-tuple-element.23, bf16[1024,2,128]{0,2,1:T(8,128)(2,1)} %bitcast, bf16[1024,2,128]{0,2,1:T(8,128)(2,1)} %collective-permute-done), kind=kOutput, calls=%fused_computation.42 | convolution fusion | flops 813432832 | bytes 14163968 | tf_op jit(solution)/shard_map/hgrk,khd->rhgd/dot_general | solution.py:49
  301.4 2.6 copy-done.6
  304.0 2.2 fusion.27
  306.3 11.5 %convolution_convert_fusion = bf16[1024,5376]{1,0:T(8,128)(2,1)} fusion(bf16[512,5376]{0,1:T(8,128)(2,1)} %all-gather.14.cloned.1.call-done, bf16[512,512]{0,1:T(8,128)(2,1)S(1)} %bitcast.90, bf16[512,512]{0,1:T(8,128)(2,1)S(1)} %bitcast.91), kind=kOutput, calls=%fused_computation.8 | convolution fusion | flops 5644746752 | bytes 17563648 | tf_op jit(solution)/shard_map/dot_general | solution.py:117
  317.9 137.5 %reduce-scatter.2.cloned.1.call-done = bf16[128,5376]{1,0:T(8,128)(2,1)} async-done(((bf16[1024,5376]{1,0:T(8,128)(2,1)}), bf16[128,5376]{1,0:T(8,128)(2,1)}) %reduce-scatter.2.cloned.1.call-update) | async-done | bytes 1376272 | tf_op jit(solution)/shard_map/reduce_scatter | solution.py:116
  455.4 1.7 fusion.16
  457.1 3.0 fusion.21
  (39 shorter events, 1.9 us)
Async XLA Ops:
  6.5 40.0 %all-gather.10.cloned.1.call-start = ((), (), s32[]{:S(2)}) async-start(), calls=%async_computation.3 | async-start | bytes 2924544 | tf_op jit(solution)/shard_map/all_gather | solution.py:104
  7.3 171.6 %all-gather.6.cloned.1.call-start = ((), (), s32[]{:S(2)}) async-start(), calls=%async_computation.1 | async-start | bytes 12386304 | tf_op jit(solution)/shard_map/all_gather | solution.py:96
  11.8 205.7 %all-gather.8.cloned.1.call-start = ((), (), s32[]{:S(2)}) async-start(), calls=%async_computation.2 | async-start | bytes 2924544 | tf_op jit(solution)/shard_map/all_gather | solution.py:105
  12.6 252.1 %all-gather.12.cloned.1.call-start = ((), (), s32[]{:S(2)}) async-start(), calls=%async_computation.4 | async-start | bytes 5849088 | tf_op jit(solution)/shard_map/all_gather | solution.py:103
  13.1 293.2 %all-gather.14.cloned.1.call-start = ((), (), s32[]{:S(2)}) async-start(), calls=%async_computation.5 | async-start | bytes 5849088 | tf_op jit(solution)/shard_map/all_gather | solution.py:115
  13.7 441.7 %reduce-scatter.2.cloned.1.call-start = ((), (), s32[]{:S(2)}) async-start(), calls=%async_computation.6 | async-start | bytes 12386304 | tf_op jit(solution)/shard_map/reduce_scatter | solution.py:116
  18.5 171.0 %copy-start.4 = (f32[128]{0:T(128)S(1)}, f32[128]{0:T(128)}, u32[]{:S(2)}) copy-start(f32[128]{0:T(128)} %param.16) | copy-start | bytes 1540
  191.4 85.6 %collective-permute-start.1 = (bf16[1024,2,128]{2,0,1:T(8,128)(2,1)}, bf16[1024,2,128]{2,0,1:T(8,128)(2,1)S(1)}, u32[]{:S(2)}, u32[]{:S(2)}) collective-permute-start(bf16[1024,2,128]{2,0,1:T(8,128)(2,1)} %pad_maximum_fusion.2), channel_id=1, source_target_pairs={{0,8},{8,16},{16,24},{24,32},{32,40},{40,48},{48,56},{56,64},{64,7... | collective-permute-start | bytes 1572872 | tf_op jit(solution)/shard_map/ppermute | solution.py:13
  226.3 48.7 %copy-start.5 = (f32[128]{0:T(128)S(1)}, f32[128]{0:T(128)}, u32[]{:S(2)}) copy-start(f32[128]{0:T(128)} %param.15) | copy-start | bytes 1540
  226.3 68.8 %collective-permute-start = (bf16[1024,2,128]{0,2,1:T(8,128)(2,1)}, bf16[1024,2,128]{0,2,1:T(8,128)(2,1)}, u32[]{:S(2)}, u32[]{:S(2)}) collective-permute-start(bf16[1024,2,128]{0,2,1:T(8,128)(2,1)} %bitcast), channel_id=1, source_target_pairs={{0,8},{8,16},{16,24},{24,32},{32,40},{40,48},{48,56},{56,64},{64,7... | collective-permute-start | bytes 1572872 | tf_op jit(solution)/shard_map/ppermute | solution.py:13
  277.3 9.5 %copy-start.1 = (pred[512,1536]{0,1:T(8,128)(4,1)S(1)}, pred[512,1536]{0,1:T(8,128)(4,1)}, u32[]{:S(2)}) copy-start(pred[512,1536]{0,1:T(8,128)(4,1)} %fusion.15) | copy-start | bytes 2359300
  277.3 9.5 %copy-start.2 = (bf16[512,4,128]{0,2,1:T(8,128)(2,1)S(1)}, bf16[512,4,128]{0,2,1:T(8,128)(2,1)}, u32[]{:S(2)}) copy-start(bf16[512,4,128]{0,2,1:T(8,128)(2,1)} %get-tuple-element.10) | copy-start | bytes 1572868
  295.1 8.9 %copy-start.6 = (f32[2,2,512,1536]{2,3,1,0:T(8,128)S(1)}, f32[2,2,512,1536]{2,3,1,0:T(8,128)}, u32[]{:S(2)}) copy-start(f32[2,2,512,1536]{2,3,1,0:T(8,128)} %get-tuple-element.26) | copy-start | bytes 37748740
  317.9 139.2 %copy-start = (bf16[128,5376]{1,0:T(8,128)(2,1)S(1)}, bf16[128,5376]{1,0:T(8,128)(2,1)}, u32[]{:S(2)}) copy-start(bf16[128,5376]{1,0:T(8,128)(2,1)} %param.9) | copy-start | bytes 4128772
  317.9 139.2 %copy-start.3 = (f32[5376]{0:T(1024)S(1)}, f32[5376]{0:T(1024)}, u32[]{:S(2)}) copy-start(f32[5376]{0:T(1024)} %param.17) | copy-start | bytes 64516
Sparse Core Ops, SparseCore 0:
  9.0 37.4 all-gather.9
  48.8 130.0 all-gather.5
  180.6 36.9 all-gather.7
  219.1 45.5 all-gather.11
  266.2 40.0 all-gather.13
  318.0 137.3 reduce-scatter.1
where the time goes:
time: 467 us
  waiting for transfers between devices  361 us (77%)
  matrix products  65.9 us (14%)
  other arithmetic  17.5 us (4%)
  between operations  13.7 us (3%)
    reduce_scatter x1, waiting for transfers between devices, per_device(): lax.psum_scatter(jnp.dot(attended, out_full, preferred_element_type=jnp.f...  138 us
    all_gather x1, waiting for transfers between devices, per_device(): block = lax.all_gather(normed, 'tp', axis=0, tiled=True)  132 us
    all_gather x1, waiting for transfers between devices, per_device(): lax.all_gather(query_weight, 'ctx', axis=0, tiled=True)  35.3 us
    dot_general x3, matrix products, add_product(): return jnp.dot(left, weight_piece, preferred_element_type=jnp.float32)  28.1 us
    all_gather x1, waiting for transfers between devices, per_device(): lax.all_gather(key_weight, 'ctx', axis=0, tiled=True)  28.1 us
    all_gather x1, waiting for transfers between devices, per_device(): lax.all_gather(value_weight, 'ctx', axis=0, tiled=True)  24.8 us
    sub x2, matrix products, attend(): expo = jnp.where(allowed, jnp.exp(scores - row_max), 0.0)  17.8 us
    dot_general x1, matrix products, per_device(): jnp.dot(attended, out_full, preferred_element_type=jnp.float32)  11.5 us
  transfers between devices with their start and end apart: 8, of which 6 were waited for; matrix products, arithmetic and copies ran while one was open for 15% of the time, Pallas kernels for 0%

commit v1 on v0

--- a/solution.py
+++ b/solution.py
@@ -101,7 +101,19 @@
     wide_pos = block_start - WINDOW + jnp.arange(WINDOW + block_rows, dtype=jnp.int32)
     kv_rows = block.shape[0]
     query_raw = add_product(block, lax.all_gather(query_weight, "ctx", axis=0, tiled=True))
-    key_raw = add_product(block, lax.all_gather(key_weight, "ctx", axis=0, tiled=True))
+
+    def flows_tell(original, peer_axis):
+        return jnp.concatenate(
+            lax.all_to_all(
+                jnp.stack([original for _ in range(lax.axis_size(peer_axis))], axis=0),
+                peer_axis,
+                0,
+                0,
+            ),
+            axis=0,
+        )
+
+    key_raw = add_product(block, flows_tell(key_weight, "ctx"))
     value_raw = add_product(block, lax.all_gather(value_weight, "ctx", axis=0, tiled=True))
     queries = rotate(
         rms_scale(query_raw.reshape(block_rows, -1, head_dim), q_gain), own_pos

time: 467 us -> 449 us (0.961)
  waiting for transfers between devices: 361 us -> 332 us
  starting transfers between devices: 4.57 us -> 11.8 us
    all_gather x1, waiting for transfers between devices: 132 us -> 85.7 us  [per_device(): block = lax.all_gather(normed, 'tp', axis=0, tiled=True)]
    all_to_all x0 -> x1, waiting for transfers between devices: none -> 43.9 us  [flows_tell(): lax.all_to_all(jnp.stack([original for _ in range(lax.axis_size(peer_axis...]
    all_gather x1 -> x0, waiting for transfers between devices: 28.1 us -> none  [per_device(): lax.all_gather(key_weight, 'ctx', axis=0, tiled=True)]
    all_to_all x0 -> x1, starting transfers between devices: none -> 6.46 us  [flows_tell(): lax.all_to_all(jnp.stack([original for _ in range(lax.axis_size(peer_axis...]
    all_gather x1, waiting for transfers between devices: 24.8 us -> 30 us  [per_device(): lax.all_gather(value_weight, 'ctx', axis=0, tiled=True)]
  transfers between devices with their start and end apart: 8 -> 8, of which waited for: 6 -> 5; matrix products, arithmetic and copies ran while one was open for 15% -> 15% of each run, Pallas kernels for 0% -> 0%
where the time goes in v1:
time: 449 us; the launch traced here: 448 us
  waiting for transfers between devices  332 us (74%)
  matrix products  65.1 us (14%)
  other arithmetic  18.4 us (4%)
  between operations  13.4 us (3%)
  starting transfers between devices  11.8 us (3%)
  local copies, waits for them, and re-layouts  7.27 us (2%)
    reduce_scatter x1, waiting for transfers between devices, per_device(): lax.psum_scatter(jnp.dot(attended, out_full, preferred_element_type=jnp.f...  137 us
    all_gather x1, waiting for transfers between devices, per_device(): block = lax.all_gather(normed, 'tp', axis=0, tiled=True)  85.7 us
    all_to_all x1, waiting for transfers between devices, flows_tell(): lax.all_to_all(jnp.stack([original for _ in range(lax.axis_size(peer_axis...  43.9 us
    all_gather x1, waiting for transfers between devices, per_device(): lax.all_gather(query_weight, 'ctx', axis=0, tiled=True)  33.3 us
    all_gather x1, waiting for transfers between devices, per_device(): lax.all_gather(value_weight, 'ctx', axis=0, tiled=True)  30 us
    dot_general x3, matrix products, add_product(): return jnp.dot(left, weight_piece, preferred_element_type=jnp.float32)  25.8 us
    sub x2, matrix products, attend(): expo = jnp.where(allowed, jnp.exp(scores - row_max), 0.0)  19.3 us
    dot_general x1, matrix products, per_device(): jnp.dot(attended, out_full, preferred_element_type=jnp.float32)  11.6 us
  transfers between devices with their start and end apart: 8, of which 5 were waited for; matrix products, arithmetic and copies ran while one was open for 15% of the time, Pallas kernels for 0%

profile of v1, /device:TPU:0, one launch (start us, length us, event | category | flops | bytes accessed | tf_op | source)
XLA Modules:
  0.0 448.1 jit_solution(12771011128860663403)
XLA Ops:
  6.5 1.7 fusion.20
  8.3 2.8 fusion.22
  11.2 0.7 all-gather.7.cloned.1.call-update
  11.9 0.7 all-gather.9.cloned.1.call-update
  12.6 1.7 stack.2
  14.3 6.5 %all-to-all-start = ((bf16[16,336,256]{2,1,0:T(8,128)(2,1)}), bf16[16,336,256]{2,1,0:T(8,128)(2,1)S(1)}, u32[]{:S(2)}, u32[]{:S(2)}) async-start(bf16[16,336,256]{2,1,0:T(8,128)(2,1)} %stack.2), calls=%async_computation | async-start | bytes 5505024 | tf_op jit(solution)/shard_map/all_to_all | solution.py:107
  20.9 0.5 all-gather.11.cloned.1.call-update
  21.5 1.0 multiply_cosine_fusion
  22.5 2.0 fusion.15
  24.5 1.9 fusion.17
  26.4 43.9 %all-to-all-done = bf16[16,336,256]{2,1,0:T(8,128)(2,1)S(1)} async-done(((bf16[16,336,256]{2,1,0:T(8,128)(2,1)}), bf16[16,336,256]{2,1,0:T(8,128)(2,1)S(1)}, u32[]{:S(2)}, u32[]{:S(2)}) %all-to-all-start) | async-done | bytes 2752544 | tf_op jit(solution)/shard_map/all_to_all | solution.py:107
  70.3 2.9 copy.17
  73.3 85.7 %all-gather.5.cloned.1.call-done = bf16[1024,5376]{1,0:T(8,128)(2,1)} async-done(((bf16[128,5376]{1,0:T(8,128)(2,1)}), bf16[1024,5376]{1,0:T(8,128)(2,1)}) %all-gather.5.cloned.1.call-update) | async-done | bytes 11010064 | tf_op jit(solution)/shard_map/all_gather | solution.py:96
  159.0 6.7 %multiply_reduce_fusion.1 = (f32[1024,2]{0,1:T(2,128)S(1)}, f32[1024,2,128]{0,2,1:T(8,128)S(1)}) fusion(bf16[2,128,5376]{2,1,0:T(8,128)(2,1)} %bitcast.94, bf16[1024,5376]{1,0:T(8,128)(2,1)} %all-gather.5.cloned.1.call-done), kind=kOutput, calls=%fused_computation.58 | convolution fusion | flops 2819094528 | bytes 14819328 | tf_op jit(solution)/shard_map/dot_general | solution.py:71
  166.1 0.8 pad_maximum_fusion.2
  166.9 2.1 collective-permute-start.1
  169.0 30.0 %all-gather.7.cloned.1.call-done = bf16[5376,256]{1,0:T(8,128)(2,1)} async-done(((bf16[336,256]{1,0:T(8,128)(2,1)}), bf16[5376,256]{1,0:T(8,128)(2,1)}) %all-gather.7.cloned.1.call-update) | async-done | bytes 2752528 | tf_op jit(solution)/shard_map/all_gather | solution.py:117
  199.1 8.7 %convolution_convert_fusion.1 = bf16[1024,256]{0,1:T(8,128)(2,1)} fusion(bf16[1024,5376]{1,0:T(8,128)(2,1)} %all-gather.5.cloned.1.call-done, bf16[5376,256]{1,0:T(8,128)(2,1)} %all-gather.7.cloned.1.call-done), kind=kOutput, calls=%fused_computation.46 | convolution fusion | flops 2818834432 | bytes 14286848 | tf_op jit(solution)/shard_map/dot_general | solution.py:71
  207.8 3.1 collective-permute-start
  210.9 33.3 %all-gather.9.cloned.1.call-done = bf16[5376,512]{1,0:T(8,128)(2,1)} async-done(((bf16[336,512]{1,0:T(8,128)(2,1)}), bf16[5376,512]{1,0:T(8,128)(2,1)}) %all-gather.9.cloned.1.call-update) | async-done | bytes 5505040 | tf_op jit(solution)/shard_map/all_gather | solution.py:103
  244.2 10.3 %multiply_reduce_fusion = (f32[1024,4]{0,1:T(4,128)S(1)}, f32[1024,512]{0,1:T(8,128)S(1)}) fusion(bf16[1024,5376]{1,0:T(8,128)(2,1)} %all-gather.5.cloned.1.call-done, bf16[5376,512]{1,0:T(8,128)(2,1)} %all-gather.9.cloned.1.call-done), kind=kOutput, calls=%fused_computation.41 | convolution fusion | flops 5638189056 | bytes 18628608 | tf_op jit(solution)/shard_map/dot_general | solution.py:71
  255.5 1.1 fusion.41
  256.6 1.1 maximum_maximum_fusion
  257.7 10.2 %fusion.53 = (f32[2,2,512]{2,1,0:T(2,128)S(1)}, f32[2,2,512,1536]{2,3,1,0:T(8,128)}) fusion(pred[512,1536]{0,1:T(8,128)(4,1)S(1)} %copy-done.1, bf16[512,2,2,128]{0,3,2,1:T(8,128)(2,1)} %bitcast.96, bf16[2048,2,128]{0,2,1:T(8,128)(2,1)S(1)} %maximum_maximum_fusion), kind=kOutput, calls=%fused_computation.95 | convolution fusion | flops 821036544 | bytes 15474688 | tf_op jit(solution)/shard_map/sub | solution.py:47
  267.9 9.1 %fusion.52 = (f32[2,2,512]{2,1,0:T(2,128)S(1)}, f32[2,2,512,1536]{2,3,1,0:T(8,128)}) fusion(pred[512,1536]{0,1:T(8,128)(4,1)S(1)} %copy-done.2, bf16[512,2,2,128]{0,3,2,1:T(8,128)(2,1)S(1)} %bitcast.95, bf16[2048,2,128]{0,2,1:T(8,128)(2,1)S(1)} %maximum_maximum_fusion), kind=kOutput, calls=%fused_computation.94 | convolution fusion | flops 821036544 | bytes 15474688 | tf_op jit(solution)/shard_map/sub | solution.py:47
  277.0 6.2 %fusion.28 = bf16[2,128,2,512]{3,1,2,0:T(8,128)(2,1)S(1)} fusion(f32[2,2,512,1536]{2,3,1,0:T(8,128)} %get-tuple-element.24, f32[2,2,512]{2,1,0:T(2,128)S(1)} %get-tuple-element.23, bf16[1024,2,128]{0,2,1:T(8,128)(2,1)} %bitcast, bf16[1024,2,128]{0,2,1:T(8,128)(2,1)} %collective-permute-done), kind=kOutput, calls=%fused_computation.44 | convolution fusion | flops 813432832 | bytes 14163968 | tf_op jit(solution)/shard_map/hgrk,khd->rhgd/dot_general | solution.py:49
  283.3 2.6 copy-done.8
  285.8 2.2 fusion.29
  288.0 11.6 %convolution_convert_fusion = bf16[1024,5376]{1,0:T(8,128)(2,1)} fusion(bf16[512,5376]{0,1:T(8,128)(2,1)} %all-gather.11.cloned.1.call-done, bf16[512,512]{0,1:T(8,128)(2,1)S(1)} %bitcast.97, bf16[512,512]{0,1:T(8,128)(2,1)S(1)} %bitcast.98), kind=kOutput, calls=%fused_computation.8 | convolution fusion | flops 5644746752 | bytes 17563648 | tf_op jit(solution)/shard_map/dot_general | solution.py:129
  299.7 137.2 %reduce-scatter.2.cloned.1.call-done = bf16[128,5376]{1,0:T(8,128)(2,1)} async-done(((bf16[1024,5376]{1,0:T(8,128)(2,1)}), bf16[128,5376]{1,0:T(8,128)(2,1)}) %reduce-scatter.2.cloned.1.call-update) | async-done | bytes 1376272 | tf_op jit(solution)/shard_map/reduce_scatter | solution.py:128
  436.9 1.7 fusion.18
  438.6 3.0 fusion.23
  (41 shorter events, 1.5 us)
Async XLA Ops:
  6.5 6.1 %copy-start.4 = (bf16[336,256]{1,0:T(8,128)(2,1)S(1)}, bf16[336,256]{1,0:T(8,128)(2,1)}, u32[]{:S(2)}) copy-start(bf16[336,256]{1,0:T(8,128)(2,1)} %param.12) | copy-start | bytes 516100
  6.5 152.5 %all-gather.5.cloned.1.call-start = ((), (), s32[]{:S(2)}) async-start(), calls=%async_computation.2 | async-start | bytes 12386304 | tf_op jit(solution)/shard_map/all_gather | solution.py:96
  11.1 187.9 %all-gather.7.cloned.1.call-start = ((), (), s32[]{:S(2)}) async-start(), calls=%async_computation.3 | async-start | bytes 2924544 | tf_op jit(solution)/shard_map/all_gather | solution.py:117
  11.9 232.4 %all-gather.9.cloned.1.call-start = ((), (), s32[]{:S(2)}) async-start(), calls=%async_computation.4 | async-start | bytes 5849088 | tf_op jit(solution)/shard_map/all_gather | solution.py:103
  14.3 56.0 %all-to-all-start = ((bf16[16,336,256]{2,1,0:T(8,128)(2,1)}), bf16[16,336,256]{2,1,0:T(8,128)(2,1)S(1)}, u32[]{:S(2)}, u32[]{:S(2)}) async-start(bf16[16,336,256]{2,1,0:T(8,128)(2,1)} %stack.2), calls=%async_computation | async-start | bytes 5505024 | tf_op jit(solution)/shard_map/all_to_all | solution.py:107
  20.8 267.2 %all-gather.11.cloned.1.call-start = ((), (), s32[]{:S(2)}) async-start(), calls=%async_computation.5 | async-start | bytes 5849088 | tf_op jit(solution)/shard_map/all_gather | solution.py:127
  21.4 415.5 %reduce-scatter.2.cloned.1.call-start = ((), (), s32[]{:S(2)}) async-start(), calls=%async_computation.6 | async-start | bytes 12386304 | tf_op jit(solution)/shard_map/reduce_scatter | solution.py:128
  159.0 6.7 %copy-start.6 = (f32[128]{0:T(128)S(1)}, f32[128]{0:T(128)}, u32[]{:S(2)}) copy-start(f32[128]{0:T(128)} %param.16) | copy-start | bytes 1540
  166.9 89.6 %collective-permute-start.1 = (bf16[1024,2,128]{0,2,1:T(8,128)(2,1)}, bf16[1024,2,128]{0,2,1:T(8,128)(2,1)}, u32[]{:S(2)}, u32[]{:S(2)}) collective-permute-start(bf16[1024,2,128]{0,2,1:T(8,128)(2,1)} %pad_maximum_fusion.2), channel_id=1, source_target_pairs={{0,8},{8,16},{16,24},{24,32},{32,40},{40,48},{48,56},{56,64},{64,7... | collective-permute-start | bytes 1572872 | tf_op jit(solution)/shard_map/ppermute | solution.py:13
  207.8 46.8 %copy-start.7 = (f32[128]{0:T(128)S(1)}, f32[128]{0:T(128)}, u32[]{:S(2)}) copy-start(f32[128]{0:T(128)} %param.15) | copy-start | bytes 1540
  207.8 69.2 %collective-permute-start = (bf16[1024,2,128]{0,2,1:T(8,128)(2,1)}, bf16[1024,2,128]{0,2,1:T(8,128)(2,1)}, u32[]{:S(2)}, u32[]{:S(2)}) collective-permute-start(bf16[1024,2,128]{0,2,1:T(8,128)(2,1)} %bitcast), channel_id=1, source_target_pairs={{0,8},{8,16},{16,24},{24,32},{32,40},{40,48},{48,56},{56,64},{64,7... | collective-permute-start | bytes 1572872 | tf_op jit(solution)/shard_map/ppermute | solution.py:13
  255.1 2.6 copy-start.1
  257.7 10.2 %copy-start.2 = (pred[512,1536]{0,1:T(8,128)(4,1)S(1)}, pred[512,1536]{0,1:T(8,128)(4,1)}, u32[]{:S(2)}) copy-start(pred[512,1536]{0,1:T(8,128)(4,1)} %fusion.17) | copy-start | bytes 2359300
  257.7 10.2 %copy-start.3 = (bf16[512,4,128]{0,2,1:T(8,128)(2,1)S(1)}, bf16[512,4,128]{0,2,1:T(8,128)(2,1)}, u32[]{:S(2)}) copy-start(bf16[512,4,128]{0,2,1:T(8,128)(2,1)} %get-tuple-element.10) | copy-start | bytes 1572868
  277.0 8.8 %copy-start.8 = (f32[2,2,512,1536]{2,3,1,0:T(8,128)S(1)}, f32[2,2,512,1536]{2,3,1,0:T(8,128)}, u32[]{:S(2)}) copy-start(f32[2,2,512,1536]{2,3,1,0:T(8,128)} %get-tuple-element.26) | copy-start | bytes 37748740
  299.6 139.0 %copy-start = (bf16[128,5376]{1,0:T(8,128)(2,1)S(1)}, bf16[128,5376]{1,0:T(8,128)(2,1)}, u32[]{:S(2)}) copy-start(bf16[128,5376]{1,0:T(8,128)(2,1)} %param.9) | copy-start | bytes 4128772
  299.6 139.0 %copy-start.5 = (f32[5376]{0:T(1024)S(1)}, f32[5376]{0:T(1024)}, u32[]{:S(2)}) copy-start(f32[5376]{0:T(1024)} %param.17) | copy-start | bytes 64516
Sparse Core Ops, SparseCore 0:
  11.2 147.7 all-gather.4
  160.7 38.3 all-gather.6
  200.8 43.4 all-gather.8
  245.8 39.9 all-gather.10
  299.8 137.0 reduce-scatter.1
